TPU v7x, 32 devices: a whole 2x2x4 slice. The times are simulated.
32 devices in a mesh: clip: 2 (over x), seq: 16 (over z, y, core).
Axes of the slice: x: 2, y: 2, z: 4, core: 2. Of those that a mesh axis runs over, the one named last changes fastest.
Arguments:
- hidden: bfloat16 [2, 1792, 1536], P(None, ('clip', 'seq')), parts along dimension 1, may hold values from -6 to 6
- latent: float32 [1792, 100], P(('clip', 'seq')), parts along dimension 0, may hold values from -6 to 6
- lengths: int32 [2], P('clip'), parts along dimension 0, may hold values from 448 to 896
- step_index: int32 [1], replicated, may hold values from 0 to 31
- guidance: float32 [1], replicated, may hold values from 1.5 to 2.5
- modulation: float32 [5, 1536], replicated, may hold values from -2.5 to 2.5
- conv_kernel: float32 [31, 1536], replicated, may hold values from -1 to 1
- w_qkv: bfloat16 [1536, 3072], replicated, may hold values from -1 to 1
- w_out: bfloat16 [1024, 1536], replicated, may hold values from -0.1875 to 0.1875
- w_mel: bfloat16 [1536, 100], replicated, may hold values from -0.15625 to 0.15625
Outputs:
- velocity: float32 [1792, 100], P(('clip', 'seq')), parts along dimension 0
- estimate: float32 [1792, 100], P(('clip', 'seq')), parts along dimension 0
There are 2 independent parts, one for each index of `clip`. A program takes and returns all parts, laid end to end along the dimension named above; an argument that names none is the same for every part. Nothing has to cross between parts.
All inputs are finite; a program needn't handle non-finite values.
Results may differ from a plain program's by a relative error of at most 0.0061.
Values may be sent and summed in bfloat16 or wider, within the bound.
No kernel may reach another device: no remote copies, remote signals or barrier semaphores. Data moves between devices by JAX's collectives and lax.ppermute only.
A program may use at most 192 MiB of HBM per device.

v0:
```python
import jax
import jax.numpy as jnp
from jax import lax
from jax.sharding import PartitionSpec as P

HEADS = 16
HEAD_DIM = 64
KERNEL = 31
STEPS = 32
EPSILON = 1e-06
NEGATIVE = -1e30


def extended(cells, sides, width):
    for axis, dim in sides:
        count = lax.axis_size(axis)
        ends = count - 1
        head = lax.slice_in_dim(cells, 0, width, axis=dim)
        tail = lax.slice_in_dim(cells, cells.shape[dim] - width, cells.shape[dim], axis=dim)
        cells = jnp.concatenate(
            [
                lax.ppermute(tail, axis, [(i, (i + 1) % count) for i in range(ends)]),
                cells,
                lax.ppermute(head, axis, [((i + 1) % count, i) for i in range(ends)]),
            ],
            axis=dim,
        )
    return cells


def from_partner(shard, axis, apart):
    return lax.ppermute(shard, axis, [(i, i ^ 1 << apart) for i in range(lax.axis_size(axis))])


def layer_norm(values, shift_row, scale_row):
    mean_value = jnp.mean(values, axis=-1, keepdims=True)
    centered = values - mean_value
    variance = jnp.mean(centered * centered, axis=-1, keepdims=True)
    return centered * lax.rsqrt(variance + EPSILON) * (1.0 + scale_row) + shift_row


def mish(values):
    return values * jnp.tanh(jax.nn.softplus(values))


def rotate(values, positions):
    half_dim = values.shape[-1] // 2
    inverse = 10000.0 ** (-jnp.arange(half_dim, dtype=jnp.float32) / half_dim)
    angles = positions.astype(jnp.float32)[:, None] * inverse[None, :]
    cosine = jnp.cos(angles)[:, None, :]
    sine_table = jnp.sin(angles)[:, None, :]
    lower_half = values[..., :half_dim]
    upper_half = values[..., half_dim:]
    return jnp.concatenate(
        [
            lower_half * cosine - upper_half * sine_table,
            upper_half * cosine + lower_half * sine_table,
        ],
        axis=-1,
    )


def to_groups(values, subs):
    copies, frame_rows, _ = values.shape
    grouped = values.reshape(copies, subs, frame_rows // subs, HEADS, HEAD_DIM).transpose(
        0, 3, 1, 2, 4
    )
    return grouped.reshape(copies * HEADS * subs, frame_rows // (2 * subs), 2 * HEAD_DIM)


def from_groups(grouped, copies, frame_rows, subs):
    split = grouped.reshape(copies, HEADS, subs, frame_rows // subs, HEAD_DIM).transpose(
        0, 2, 3, 1, 4
    )
    return split.reshape(copies, frame_rows, HEADS * HEAD_DIM)


def block_size_for(row_total):
    for candidate in range(1024, 7, -8):
        if row_total % candidate == 0:
            return candidate
    return row_total


def attend_local(query_flat, key_flat, value_flat, key_live):
    groups, query_total, _ = query_flat.shape
    block_rows = block_size_for(query_total)
    blocks = query_flat.reshape(groups, query_total // block_rows, block_rows, HEAD_DIM).transpose(
        1, 0, 2, 3
    )
    scale_factor = HEAD_DIM ** (-0.5)
    live_mask = key_live[None, None, :]

    def one_block(block):
        scores = (
            jnp.einsum("gqd,gkd->gqk", block, key_flat, preferred_element_type=jnp.float32)
            * scale_factor
        )
        scores = jnp.where(live_mask, scores, NEGATIVE)
        row_peak = jnp.max(scores, axis=-1, keepdims=True)
        weights = jnp.where(live_mask, jnp.exp(scores - row_peak), 0.0)
        weight_sum = jnp.sum(weights, axis=-1)
        weighted = jnp.einsum(
            "gqk,gkd->gqd",
            weights.astype(jnp.bfloat16),
            value_flat,
            preferred_element_type=jnp.float32,
        )
        return (weighted / weight_sum[..., None]).astype(jnp.bfloat16)

    results = lax.map(one_block, blocks)
    return results.transpose(1, 0, 2, 3).reshape(groups, query_total, HEAD_DIM)


def per_device(
    hidden, latent, lengths, step_index, guidance, modulation, conv_kernel, w_qkv, w_out, w_mel
):
    copies, frame_rows, model_width = hidden.shape
    offset = lax.axis_index("seq") * frame_rows
    positions = offset + jnp.arange(frame_rows, dtype=jnp.int32)
    length = lengths[0]
    is_live = positions < length
    masked = hidden * is_live[None, :, None].astype(jnp.bfloat16)
    half_width = KERNEL // 2
    padded = extended(masked, (("seq", 1),), half_width)
    convolved = jnp.zeros(hidden.shape, jnp.float32)
    for tap_index in range(KERNEL):
        convolved = convolved + conv_kernel[tap_index] * padded[
            :, tap_index : tap_index + frame_rows, :
        ].astype(jnp.float32)
    residual = hidden.astype(jnp.float32) + mish(convolved)
    normed = layer_norm(residual, modulation[0], modulation[1]).astype(jnp.bfloat16)
    projected = jnp.dot(normed.reshape(-1, model_width), w_qkv, preferred_element_type=jnp.float32)
    projected = projected.reshape(copies, frame_rows, 3, HEADS, HEAD_DIM)
    queries = rotate(projected[:, :, 0], positions).astype(jnp.bfloat16)
    keys_all = (
        rotate(projected[:, :, 1], positions)
        .astype(jnp.bfloat16)
        .reshape(copies, frame_rows, HEADS * HEAD_DIM)
    )
    values_all = (
        projected[:, :, 2].astype(jnp.bfloat16).reshape(copies, frame_rows, HEADS * HEAD_DIM)
    )
    seq_size = lax.axis_size("seq")
    subs = max(1, seq_size // (2 * HEADS))
    sub_index = lax.axis_index("seq") % subs
    part_rows = frame_rows // subs
    queries_flat = queries.reshape(copies, frame_rows, HEADS * HEAD_DIM)
    sent = (to_groups(queries_flat, subs), to_groups(keys_all, subs), to_groups(values_all, subs))
    query_group, key_group, value_group = (
        lax.all_to_all(sent[0], "seq", split_axis=0, concat_axis=1, tiled=True),
        lax.all_to_all(sent[1], "seq", split_axis=0, concat_axis=1, tiled=True),
        lax.all_to_all(sent[2], "seq", split_axis=0, concat_axis=1, tiled=True),
    )

    def key_positions(sub_id):
        source_start = jnp.arange(seq_size, dtype=jnp.int32)[:, None] * frame_rows
        return (
            source_start + sub_id * part_rows + jnp.arange(part_rows, dtype=jnp.int32)[None, :]
        ).reshape(-1)

    key_rows = key_positions(sub_index)
    if subs > 1:
        other_keys, other_values = from_partner((key_group, value_group), "seq", 0)
        key_group = jnp.concatenate([key_group, other_keys], axis=1)
        value_group = jnp.concatenate([value_group, other_values], axis=1)
        key_rows = jnp.concatenate([key_rows, key_positions(1 - sub_index)])
    groups = query_group.shape[0]
    query_flat = query_group.reshape(groups, -1, HEAD_DIM)
    key_flat = key_group.reshape(groups, -1, HEAD_DIM)
    value_flat = value_group.reshape(groups, -1, HEAD_DIM)
    attended_group = attend_local(query_flat, key_flat, value_flat, key_rows < length)
    returned = lax.all_to_all(
        attended_group.reshape(groups, -1, 2 * HEAD_DIM),
        "seq",
        split_axis=1,
        concat_axis=0,
        tiled=True,
    )
    attended = from_groups(returned, copies, frame_rows, subs)
    branch = jnp.dot(
        attended.reshape(copies * frame_rows, -1), w_out, preferred_element_type=jnp.float32
    )
    after = residual + modulation[2] * branch.reshape(copies, frame_rows, model_width)
    final_norm = layer_norm(after, modulation[3], modulation[4]).astype(jnp.bfloat16)
    speed = jnp.dot(final_norm.reshape(-1, model_width), w_mel, preferred_element_type=jnp.float32)
    speed = speed.reshape(copies, frame_rows, -1)
    guided = speed[0] + guidance[0] * (speed[0] - speed[1])
    velocity = jnp.where(is_live[:, None], guided, 0.0)
    progress = step_index[0].astype(jnp.float32) / STEPS
    time_now = 1.0 - jnp.cos(0.5 * jnp.pi * progress)
    estimate = latent + (1.0 - time_now) * velocity
    return (velocity, estimate)


def solution(mesh):
    return jax.shard_map(
        per_device,
        mesh=mesh,
        in_specs=(
            P(None, ("clip", "seq"), None),
            P(("clip", "seq"), None),
            P("clip"),
            P(),
            P(),
            P(),
            P(),
            P(),
            P(),
            P(),
        ),
        out_specs=(P(("clip", "seq"), None), P(("clip", "seq"), None)),
        check_vma=False,
    )
```

profile of v0, /device:TPU:0, one launch (start us, length us, event | category | flops | bytes accessed | tf_op | source)
XLA Modules:
  0.0 131.8 jit_solution(2257580926688157541)
XLA Ops:
  1.5 1.2 broadcast_multiply_fusion
  2.7 0.7 fusion.78
  3.4 3.0 %collective-permute-start = (bf16[2,15,1536]{2,1,0:T(8,128)(2,1)}, bf16[2,15,1536]{2,1,0:T(8,128)(2,1)}, u32[]{:S(2)}, u32[]{:S(2)}) collective-permute-start(bf16[2,15,1536]{2,1,0:T(8,128)(2,1)} %get-tuple-element.74), channel_id=1, source_target_pairs={{0,1},{1,2},{2,3},{3,4},{4,5},{5,6},{6,7},{7,8},{8,9},{9,10},{10,1... | collective-permute-start | bytes 276488 | tf_op jit(solution)/shard_map/ppermute | solution.py:22
  6.4 1.3 collective-permute-start.1
  7.7 2.5 %slice_reduce_fusion.33 = (f32[1536]{0:T(1024)S(1)}, f32[1536]{0:T(1024)S(1)}, f32[1536]{0:T(1024)S(1)}, f32[1536]{0:T(1024)S(1)}, f32[1536]{0:T(1024)S(1)}, /*i...) fusion(f32[31,1536]{1,0:T(8,128)} %param.16), kind=kLoop, calls=%fused_computation.177 | loop fusion | bytes 233472 | tf_op jit(solution)/shard_map/slice | solution.py:128
  10.2 2.1 %slice_reduce_fusion.32 = (f32[1536]{0:T(1024)}, f32[1536]{0:T(1024)}, f32[1536]{0:T(1024)}, f32[1536]{0:T(1024)}, f32[1536]{0:T(1024)}, /*index=5*/f32[1536]{0:...) fusion(f32[31,1536]{1,0:T(8,128)} %param.16), kind=kLoop, calls=%fused_computation.176 | loop fusion | bytes 147456 | tf_op jit(solution)/shard_map/slice | solution.py:128
  12.3 12.7 %copy.34 = bf16[1536,3072]{0,1:T(8,128)(2,1)} copy(bf16[1536,3072]{1,0:T(8,128)(2,1)} %param.17) | data formatting | bytes 18874368 | tf_op args[7]
  25.2 1.7 %add_reduce_fusion = (f32[1536]{0:T(1024)S(1)}, f32[1536]{0:T(1024)S(1)}, f32[1536]{0:T(1024)S(1)}, f32[1536]{0:T(1024)}, f32[1536]{0:T(1024)}) fusion(f32[5,1536]{1,0:T(8,128)} %param.15), kind=kLoop, calls=%fused_computation.143 | loop fusion | flops 3072 | bytes 61440 | tf_op jit(solution)/shard_map/add | solution.py:39
  26.9 8.2 %fusion.74 = (f32[2,56]{1,0:T(2,128)S(1)}, f32[2,56,1536]{2,1,0:T(8,128)S(1)}) fusion(bf16[2,15,1536]{2,1,0:T(8,128)(2,1)} %collective-permute-done.1, bf16[2,56,1536]{2,1,0:T(8,128)(2,1)S(1)} %broadcast_multiply_fusion, f32[1536]{0:T(1024)} %get-tuple-element.55, f32[1536]{0:T(1024)} %get-tuple-element.56, f32[1536]{0:T(1024)S(1)} %get-tuple-element.27, ...), kind=kLoop, calls=%fused_computation.189 | loop fusion | flops 33030032 | bytes 1751488 | tf_op jit(solution)/shard_map/reduce_sum | solution.py:36
  35.2 0.2 multiply_reduce_fusion.1
  35.4 7.3 %fusion.60 = f32[2,56,3,16,64]{4,1,3,2,0:T(8,128)S(1)} fusion(bf16[3,16,64,1536,1]{3,2,1,0,4:T(8,128)(2,1)} %bitcast.90, f32[2,56,1536]{2,1,0:T(8,128)S(1)} %get-tuple-element.65, f32[1536]{0:T(1024)S(1)} %get-tuple-element.58, f32[1536]{0:T(1024)S(1)} %get-tuple-element.59, f32[2,56]{1,0:T(2,128)S(1)} %add_rsqrt_fusion.1, ...), kind=kOutput, calls=%fused_computation.123 | convolution fusion | flops 1057824768 | bytes 11514752 | tf_op jit(solution)/shard_map/dot_general | solution.py:133
  42.9 1.7 %fusion.28 = (bf16[2,1,56,16,32]{4,2,3,0,1:T(8,128)(2,1)S(1)}, bf16[2,1,56,16,32]{4,2,3,0,1:T(8,128)(2,1)S(1)}, bf16[2,1,56,16,32]{4,2,3,0,1:T(8,128)(2,1)}, bf16[2,1,56,16,32]{4,2,3,0,1:T(8,128)(2,1)}) fusion(f32[2,56,16,64]{3,1,2,0:T(8,128)S(1)} %get-tuple-element.68, f32[56,32]{1,0:T(8,128)S(1)} %get-tuple-element.79, f32[56,32]{1,0:T(8,128)S(1)} %get-tuple-element.78, ...), kind=kLoop, calls=%fused_computation.61 | loop fusion | flops 917504 | bytes 1390592 | tf_op jit(solution)/shard_map/concatenate | solution.py:54
  44.5 1.0 maximum_bitcast_fusion.1
  45.6 2.0 %reshape.294 = bf16[32,28,128]{2,1,0:T(8,128)(2,1)} reshape(bf16[2,16,1,56,64]{4,3,1,0,2:T(8,128)(2,1)} %maximum_bitcast_fusion.1) | data formatting | bytes 458752 | tf_op jit(solution)/shard_map/reshape | solution.py:68
  47.5 8.7 %all-to-all-start.1 = ((bf16[32,28,128]{2,1,0:T(8,128)(2,1)}), bf16[32,28,128]{2,1,0:T(8,128)(2,1)S(1)}, u32[]{:S(2)}, u32[]{:S(2)}) async-start(bf16[32,28,128]{2,1,0:T(8,128)(2,1)} %reshape.294), calls=%async_computation.1 | async-start | bytes 524288 | tf_op jit(solution)/shard_map/all_to_all | solution.py:152
  56.2 2.2 %maximum_bitcast_fusion = bf16[2,16,1,56,64]{4,3,1,0,2:T(8,128)(2,1)} fusion(bf16[2,1,56,16,32]{4,2,3,0,1:T(8,128)(2,1)} %get-tuple-element.76, bf16[2,1,56,16,32]{4,2,3,0,1:T(8,128)(2,1)} %get-tuple-element.77), kind=kLoop, calls=%fused_computation.64 | loop fusion | flops 458752 | bytes 458752 | tf_op jit(solution)/shard_map/transpose | solution.py:65
  58.4 2.0 %reshape.293 = bf16[32,28,128]{2,1,0:T(8,128)(2,1)} reshape(bf16[2,16,1,56,64]{4,3,1,0,2:T(8,128)(2,1)} %maximum_bitcast_fusion) | data formatting | bytes 458752 | tf_op jit(solution)/shard_map/reshape | solution.py:68
  60.4 5.9 %all-to-all-done.1 = bf16[32,28,128]{2,1,0:T(8,128)(2,1)S(1)} async-done(((bf16[32,28,128]{2,1,0:T(8,128)(2,1)}), bf16[32,28,128]{2,1,0:T(8,128)(2,1)S(1)}, u32[]{:S(2)}, u32[]{:S(2)}) %all-to-all-start.1) | async-done | bytes 229408 | tf_op jit(solution)/shard_map/all_to_all | solution.py:152
  66.2 4.2 %all-to-all-start = ((bf16[32,28,128]{2,1,0:T(8,128)(2,1)}), bf16[32,28,128]{2,1,0:T(8,128)(2,1)}, u32[]{:S(2)}, u32[]{:S(2)}) async-start(bf16[32,28,128]{2,1,0:T(8,128)(2,1)} %reshape.293), calls=%async_computation | async-start | bytes 524288 | tf_op jit(solution)/shard_map/all_to_all | solution.py:151
  70.4 2.0 %fusion.30 = bf16[2,16,1,56,64]{4,3,1,0,2:T(8,128)(2,1)} fusion(f32[2,56,3,16,64]{4,1,3,2,0:T(8,128)} %copy-done.2), kind=kLoop, calls=%fused_computation.63 | loop fusion | bytes 458752 | tf_op jit(solution)/shard_map/transpose | solution.py:65
  72.5 2.0 %reshape.296 = bf16[32,28,128]{2,1,0:T(8,128)(2,1)} reshape(bf16[2,16,1,56,64]{4,3,1,0,2:T(8,128)(2,1)} %fusion.30) | data formatting | bytes 458752 | tf_op jit(solution)/shard_map/reshape | solution.py:68
  74.4 6.0 %all-to-all-done = bf16[32,28,128]{2,1,0:T(8,128)(2,1)} async-done(((bf16[32,28,128]{2,1,0:T(8,128)(2,1)}), bf16[32,28,128]{2,1,0:T(8,128)(2,1)}, u32[]{:S(2)}, u32[]{:S(2)}) %all-to-all-start) | async-done | bytes 229408 | tf_op jit(solution)/shard_map/all_to_all | solution.py:151
  80.4 4.4 %all-to-all-start.2 = ((bf16[32,28,128]{2,1,0:T(8,128)(2,1)}), bf16[32,28,128]{2,1,0:T(8,128)(2,1)}, u32[]{:S(2)}, u32[]{:S(2)}) async-start(bf16[32,28,128]{2,1,0:T(8,128)(2,1)} %reshape.296), calls=%async_computation.2 | async-start | bytes 524288 | tf_op jit(solution)/shard_map/all_to_all | solution.py:153
  85.0 0.7 copy.60
  85.7 2.0 %reshape.295 = bf16[2,896,64]{2,1,0:T(8,128)(2,1)} reshape(bf16[2,16,28,128]{3,2,1,0:T(8,128)(2,1)} %bitcast.94) | data formatting | bytes 458752 | tf_op jit(solution)/shard_map/reshape | solution.py:170
  87.7 1.0 copy.61
  88.7 1.0 squeeze.26
  89.7 4.9 %all-to-all-done.2 = bf16[32,28,128]{2,1,0:T(8,128)(2,1)} async-done(((bf16[32,28,128]{2,1,0:T(8,128)(2,1)}), bf16[32,28,128]{2,1,0:T(8,128)(2,1)}, u32[]{:S(2)}, u32[]{:S(2)}) %all-to-all-start.2) | async-done | bytes 229408 | tf_op jit(solution)/shard_map/all_to_all | solution.py:153
  94.7 1.0 copy.59
  95.6 1.0 reshape.297
  96.6 5.7 %fusion.79 = (f32[2,896]{1,0:T(2,128)S(1)}, bf16[2,896,896]{1,2,0:T(8,128)(2,1)}) fusion(pred[896]{0:T(1024)(128)(4,1)S(1)} %lt.36, bf16[2,896,64]{2,1,0:T(8,128)(2,1)} %squeeze.26, bf16[2,896,64]{2,1,0:T(8,128)(2,1)} %reshape.295), kind=kOutput, calls=%fused_computation.192 | convolution fusion | flops 215155584 | bytes 3678080 | tf_op jit(solution)/shard_map/while/body/eval_jaxpr/sub | solution.py:101
  102.4 2.7 %fusion.18 = bf16[2,896,64]{1,2,0:T(8,128)(2,1)S(1)} fusion(bf16[2,896,64]{2,1,0:T(8,128)(2,1)} %reshape.297, bf16[2,896,896]{1,2,0:T(8,128)(2,1)} %get-tuple-element.81, f32[2,896]{1,0:T(2,128)S(1)} %get-tuple-element.80), kind=kOutput, calls=%fused_computation.43 | convolution fusion | flops 205750272 | bytes 3677184 | tf_op jit(solution)/shard_map/while/body/eval_jaxpr/gqk,gkd->gqd/dot_general | solution.py:103
  105.0 1.0 copy.43
  106.0 1.3 reshape_reshape_transpose.3
  107.3 0.9 copy.44
  108.2 3.5 %all-to-all-start.3 = ((bf16[2,448,128]{2,0,1:T(2,128)(2,1)}), bf16[2,448,128]{2,0,1:T(2,128)(2,1)S(1)}, u32[]{:S(2)}, u32[]{:S(2)}) async-start(bf16[2,448,128]{2,0,1:T(2,128)(2,1)} %copy.44), calls=%async_computation.3 | async-start | bytes 458752 | tf_op jit(solution)/shard_map/all_to_all | solution.py:173
  113.2 8.0 %all-to-all-done.3 = bf16[2,448,128]{2,0,1:T(2,128)(2,1)S(1)} async-done(((bf16[2,448,128]{2,0,1:T(2,128)(2,1)}), bf16[2,448,128]{2,0,1:T(2,128)(2,1)S(1)}, u32[]{:S(2)}, u32[]{:S(2)}) %all-to-all-start.3) | async-done | bytes 229408 | tf_op jit(solution)/shard_map/all_to_all | solution.py:173
  121.2 0.7 copy-done.3
  121.9 1.0 copy.45
  122.8 1.0 reshape.298
  123.9 1.9 %copy.46 = bf16[2,1,56,16,64]{4,3,2,0,1:T(8,128)(2,1)} copy(bf16[2,1,56,16,64]{4,2,3,0,1:T(8,128)(2,1)} %bitcast.91) | data formatting | bytes 458752 | tf_op jit(solution)/shard_map/transpose | solution.py:72
  125.7 1.4 %dot_general.28 = bf16[2,56,1024]{2,1,0:T(8,128)(2,1)S(1)} reshape(bf16[2,1,56,16,64]{4,3,2,0,1:T(8,128)(2,1)} %copy.46) | data formatting | bytes 458752 | tf_op jit(solution)/shard_map/dot_general | solution.py:181
  127.1 1.8 %fusion.80 = (f32[2,56]{1,0:T(2,128)S(1)}, f32[2,56,1536]{2,1,0:T(8,128)S(1)}) fusion(f32[2,56,1536]{2,1,0:T(8,128)} %copy-done.1, bf16[2,56,1024]{2,1,0:T(8,128)(2,1)S(1)} %dot_general.28, bf16[1024,1536]{1,0:T(8,128)(2,1)S(1)} %copy-done, f32[1536]{0:T(1024)S(1)} %copy-done.5), kind=kOutput, calls=%fused_computation.193 | convolution fusion | flops 352837504 | bytes 4757952 | tf_op jit(solution)/shard_map/dot_general | solution.py:181
  129.0 0.2 multiply_reduce_fusion
  129.2 0.9 add_convert_fusion.2
  130.1 0.2 fusion.81
  130.5 0.7 copy.48
  131.1 0.7 copy.49
  (29 shorter events, 0.8 us)
Async XLA Ops:
  0.6 126.5 %copy-start = (bf16[1024,1536]{1,0:T(8,128)(2,1)S(1)}, bf16[1024,1536]{1,0:T(8,128)(2,1)}, u32[]{:S(2)}) copy-start(bf16[1024,1536]{1,0:T(8,128)(2,1)} %param.18) | copy-start | bytes 9437188
  3.4 23.6 %collective-permute-start = (bf16[2,15,1536]{2,1,0:T(8,128)(2,1)}, bf16[2,15,1536]{2,1,0:T(8,128)(2,1)}, u32[]{:S(2)}, u32[]{:S(2)}) collective-permute-start(bf16[2,15,1536]{2,1,0:T(8,128)(2,1)} %get-tuple-element.74), channel_id=1, source_target_pairs={{0,1},{1,2},{2,3},{3,4},{4,5},{5,6},{6,7},{7,8},{8,9},{9,10},{10,1... | collective-permute-start | bytes 276488 | tf_op jit(solution)/shard_map/ppermute | solution.py:22
  6.4 20.5 %collective-permute-start.1 = (bf16[2,15,1536]{2,1,0:T(8,128)(2,1)}, bf16[2,15,1536]{2,1,0:T(8,128)(2,1)}, u32[]{:S(2)}, u32[]{:S(2)}) collective-permute-start(bf16[2,15,1536]{2,1,0:T(8,128)(2,1)} %get-tuple-element.75), channel_id=1, source_target_pairs={{1,0},{2,1},{3,2},{4,3},{5,4},{6,5},{7,6},{8,7},{9,8},{10,9},{11,1... | collective-permute-start | bytes 276488 | tf_op jit(solution)/shard_map/ppermute | solution.py:24
  35.2 7.5 %copy-start.1 = (f32[2,56,1536]{2,1,0:T(8,128)}, f32[2,56,1536]{2,1,0:T(8,128)S(1)}, u32[]{:S(2)}) copy-start(f32[2,56,1536]{2,1,0:T(8,128)S(1)} %get-tuple-element.65) | copy-start | bytes 2064388
  42.7 1.8 %copy-start.2 = (f32[2,56,3,16,64]{4,1,3,2,0:T(8,128)}, f32[2,56,3,16,64]{4,1,3,2,0:T(8,128)S(1)}, u32[]{:S(2)}) copy-start(f32[2,56,3,16,64]{4,1,3,2,0:T(8,128)S(1)} %fusion.60) | copy-start | bytes 4128772
  47.5 18.7 %all-to-all-start.1 = ((bf16[32,28,128]{2,1,0:T(8,128)(2,1)}), bf16[32,28,128]{2,1,0:T(8,128)(2,1)S(1)}, u32[]{:S(2)}, u32[]{:S(2)}) async-start(bf16[32,28,128]{2,1,0:T(8,128)(2,1)} %reshape.294), calls=%async_computation.1 | async-start | bytes 524288 | tf_op jit(solution)/shard_map/all_to_all | solution.py:152
  66.2 14.2 %all-to-all-start = ((bf16[32,28,128]{2,1,0:T(8,128)(2,1)}), bf16[32,28,128]{2,1,0:T(8,128)(2,1)}, u32[]{:S(2)}, u32[]{:S(2)}) async-start(bf16[32,28,128]{2,1,0:T(8,128)(2,1)} %reshape.293), calls=%async_computation | async-start | bytes 524288 | tf_op jit(solution)/shard_map/all_to_all | solution.py:151
  80.4 14.2 %all-to-all-start.2 = ((bf16[32,28,128]{2,1,0:T(8,128)(2,1)}), bf16[32,28,128]{2,1,0:T(8,128)(2,1)}, u32[]{:S(2)}, u32[]{:S(2)}) async-start(bf16[32,28,128]{2,1,0:T(8,128)(2,1)} %reshape.296), calls=%async_computation.2 | async-start | bytes 524288 | tf_op jit(solution)/shard_map/all_to_all | solution.py:153
  102.4 9.4 %copy-start.6 = (f32[56,100]{1,0:T(8,128)S(1)}, f32[56,100]{1,0:T(8,128)}, u32[]{:S(2)}) copy-start(f32[56,100]{1,0:T(8,128)} %param.11) | copy-start | bytes 67204
  102.4 24.8 %copy-start.5 = (f32[1536]{0:T(1024)S(1)}, f32[1536]{0:T(1024)}, u32[]{:S(2)}) copy-start(f32[1536]{0:T(1024)} %get-tuple-element.60) | copy-start | bytes 18436
  108.2 13.0 %all-to-all-start.3 = ((bf16[2,448,128]{2,0,1:T(2,128)(2,1)}), bf16[2,448,128]{2,0,1:T(2,128)(2,1)S(1)}, u32[]{:S(2)}, u32[]{:S(2)}) async-start(bf16[2,448,128]{2,0,1:T(2,128)(2,1)} %copy.44), calls=%async_computation.3 | async-start | bytes 458752 | tf_op jit(solution)/shard_map/all_to_all | solution.py:173
  121.2 0.7 copy-start.3
  127.1 3.0 %copy-start.4 = (bf16[1536,100]{0,1:T(8,128)(2,1)S(1)}, bf16[1536,100]{0,1:T(8,128)(2,1)}, u32[]{:S(2)}) copy-start(bf16[1536,100]{0,1:T(8,128)(2,1)} %param.19) | copy-start | bytes 921604
where the time goes:
time: 134 us; the launch traced here: 132 us
  local copies, waits for them, and re-layouts  43.5 us (32%)
  starting transfers between devices  25.1 us (19%)
  waiting for transfers between devices  24.8 us (19%)
  other arithmetic  17.8 us (13%)
  matrix products  17.7 us (13%)
  between operations  3.05 us (2%)
    unnamed x18, local copies, waits for them, and re-layouts  14.9 us
    all_to_all x1, starting transfers between devices, per_device(): lax.all_to_all(sent[1], 'seq', split_axis=0, concat_axis=1, tiled=True)  8.67 us
    reduce_sum x1, other arithmetic, layer_norm(): mean_value = jnp.mean(values, axis=-1, keepdims=True)  8.24 us
    all_to_all x1, waiting for transfers between devices, per_device(): lax.all_to_all(attended_group.reshape(groups, -1, 2 * HEAD_DIM), 'seq', s...  7.96 us
    dot_general x1, matrix products, per_device(): jnp.dot(normed.reshape(-1, model_width), w_qkv, preferred_element_type=jn...  7.27 us
    all_to_all x1, waiting for transfers between devices, per_device(): lax.all_to_all(sent[0], 'seq', split_axis=0, concat_axis=1, tiled=True)  6.01 us
    reshape x3, local copies, waits for them, and re-layouts, to_groups(): grouped.reshape(copies * HEADS * subs, frame_rows // (2 * subs), 2 * HEAD...  5.91 us
    all_to_all x1, waiting for transfers between devices, per_device(): lax.all_to_all(sent[1], 'seq', split_axis=0, concat_axis=1, tiled=True)  5.86 us
  transfers between devices with their start and end apart: 6, of which 4 were waited for; matrix products, arithmetic and copies ran while one was open for 25% of the time, Pallas kernels for 0%

commit v1 on v0

--- a/solution.py
+++ b/solution.py
@@ -170,12 +170,18 @@
     key_flat = key_group.reshape(groups, -1, HEAD_DIM)
     value_flat = value_group.reshape(groups, -1, HEAD_DIM)
     attended_group = attend_local(query_flat, key_flat, value_flat, key_rows < length)
-    returned = lax.all_to_all(
-        attended_group.reshape(groups, -1, 2 * HEAD_DIM),
-        "seq",
-        split_axis=1,
-        concat_axis=0,
-        tiled=True,
+    returned = jnp.concatenate(
+        lax.all_to_all(
+            jnp.stack(
+                jnp.split(
+                    attended_group.reshape(groups, -1, 2 * HEAD_DIM), lax.axis_size("seq"), axis=1
+                )
+            ),
+            "seq",
+            0,
+            0,
+        ),
+        axis=0,
     )
     attended = from_groups(returned, copies, frame_rows, subs)
     branch = jnp.dot(

time: 134 us -> 134 us (level)
    another operation x0 -> x3, local copies, waits for them, and re-layouts: none -> 1.89 us  [the longest x1 1.01 us: from_groups(): grouped.reshape(copies, HEADS, subs, frame_rows // subs, HEAD_DIM)]
    unnamed x18 -> x31, local copies, waits for them, and re-layouts: 14.9 us -> 14.4 us
where the time goes in v1:
time: 134 us; the launch traced here: 132 us
  local copies, waits for them, and re-layouts  43 us (32%)
  starting transfers between devices  25.7 us (19%)
  waiting for transfers between devices  24.8 us (19%)
  other arithmetic  17.8 us (13%)
  matrix products  17.7 us (13%)
  between operations  3.12 us (2%)
    unnamed x31, local copies, waits for them, and re-layouts  14.4 us
    all_to_all x1, starting transfers between devices, per_device(): lax.all_to_all(sent[1], 'seq', split_axis=0, concat_axis=1, tiled=True)  8.67 us
    reduce_sum x1, other arithmetic, layer_norm(): mean_value = jnp.mean(values, axis=-1, keepdims=True)  8.24 us
    all_to_all x1, waiting for transfers between devices, per_device(): lax.all_to_all(jnp.stack(jnp.split(attended_group.reshape(groups, -1, 2 *...  8.01 us
    dot_general x1, matrix products, per_device(): jnp.dot(normed.reshape(-1, model_width), w_qkv, preferred_element_type=jn...  7.27 us
    all_to_all x1, waiting for transfers between devices, per_device(): lax.all_to_all(sent[0], 'seq', split_axis=0, concat_axis=1, tiled=True)  6.01 us
    reshape x3, local copies, waits for them, and re-layouts, to_groups(): grouped.reshape(copies * HEADS * subs, frame_rows // (2 * subs), 2 * HEAD...  5.91 us
    all_to_all x1, waiting for transfers between devices, per_device(): lax.all_to_all(sent[1], 'seq', split_axis=0, concat_axis=1, tiled=True)  5.86 us
  transfers between devices with their start and end apart: 6, of which 4 were waited for; matrix products, arithmetic and copies ran while one was open for 25% of the time, Pallas kernels for 0%

profile of v1, /device:TPU:0, one launch (start us, length us, event | category | flops | bytes accessed | tf_op | source)
XLA Modules:
  0.0 132.1 jit_solution(2915310834250251281)
XLA Ops:
  1.5 1.2 broadcast_multiply_fusion
  2.7 0.7 fusion.78
  3.4 3.0 %collective-permute-start = (bf16[2,15,1536]{2,1,0:T(8,128)(2,1)}, bf16[2,15,1536]{2,1,0:T(8,128)(2,1)}, u32[]{:S(2)}, u32[]{:S(2)}) collective-permute-start(bf16[2,15,1536]{2,1,0:T(8,128)(2,1)} %get-tuple-element.74), channel_id=1, source_target_pairs={{0,1},{1,2},{2,3},{3,4},{4,5},{5,6},{6,7},{7,8},{8,9},{9,10},{10,1... | collective-permute-start | bytes 276488 | tf_op jit(solution)/shard_map/ppermute | solution.py:22
  6.4 1.3 collective-permute-start.1
  7.7 2.5 %slice_reduce_fusion.33 = (f32[1536]{0:T(1024)S(1)}, f32[1536]{0:T(1024)S(1)}, f32[1536]{0:T(1024)S(1)}, f32[1536]{0:T(1024)S(1)}, f32[1536]{0:T(1024)S(1)}, /*i...) fusion(f32[31,1536]{1,0:T(8,128)} %param.16), kind=kLoop, calls=%fused_computation.209 | loop fusion | bytes 233472 | tf_op jit(solution)/shard_map/slice | solution.py:128
  10.2 2.1 %slice_reduce_fusion.32 = (f32[1536]{0:T(1024)}, f32[1536]{0:T(1024)}, f32[1536]{0:T(1024)}, f32[1536]{0:T(1024)}, f32[1536]{0:T(1024)}, /*index=5*/f32[1536]{0:...) fusion(f32[31,1536]{1,0:T(8,128)} %param.16), kind=kLoop, calls=%fused_computation.208 | loop fusion | bytes 147456 | tf_op jit(solution)/shard_map/slice | solution.py:128
  12.3 12.7 %copy.32 = bf16[1536,3072]{0,1:T(8,128)(2,1)} copy(bf16[1536,3072]{1,0:T(8,128)(2,1)} %param.17) | data formatting | bytes 18874368 | tf_op args[7]
  25.1 0.2 multiply_cosine_fusion
  25.2 1.7 %add_reduce_fusion = (f32[1536]{0:T(1024)S(1)}, f32[1536]{0:T(1024)S(1)}, f32[1536]{0:T(1024)S(1)}, f32[1536]{0:T(1024)}, f32[1536]{0:T(1024)}) fusion(f32[5,1536]{1,0:T(8,128)} %param.15), kind=kLoop, calls=%fused_computation.175 | loop fusion | flops 3072 | bytes 61440 | tf_op jit(solution)/shard_map/add | solution.py:39
  26.9 8.2 %fusion.74 = (f32[2,56]{1,0:T(2,128)S(1)}, f32[2,56,1536]{2,1,0:T(8,128)S(1)}) fusion(bf16[2,15,1536]{2,1,0:T(8,128)(2,1)} %collective-permute-done.1, bf16[2,56,1536]{2,1,0:T(8,128)(2,1)S(1)} %broadcast_multiply_fusion, f32[1536]{0:T(1024)} %get-tuple-element.55, f32[1536]{0:T(1024)} %get-tuple-element.56, f32[1536]{0:T(1024)S(1)} %get-tuple-element.27, ...), kind=kLoop, calls=%fused_computation.221 | loop fusion | flops 33030032 | bytes 1751488 | tf_op jit(solution)/shard_map/reduce_sum | solution.py:36
  35.2 0.2 multiply_reduce_fusion.1
  35.4 7.3 %fusion.60 = f32[2,56,3,16,64]{4,1,3,2,0:T(8,128)S(1)} fusion(bf16[3,16,64,1536,1]{3,2,1,0,4:T(8,128)(2,1)} %bitcast.151, f32[2,56,1536]{2,1,0:T(8,128)S(1)} %get-tuple-element.65, f32[1536]{0:T(1024)S(1)} %get-tuple-element.58, f32[1536]{0:T(1024)S(1)} %get-tuple-element.59, f32[2,56]{1,0:T(2,128)S(1)} %add_rsqrt_fusion.1, ...), kind=kOutput, calls=%fused_computation.123 | convolution fusion | flops 1057824768 | bytes 11514752 | tf_op jit(solution)/shard_map/dot_general | solution.py:133
  42.9 1.7 %fusion.28 = (bf16[2,1,56,16,32]{4,2,3,0,1:T(8,128)(2,1)S(1)}, bf16[2,1,56,16,32]{4,2,3,0,1:T(8,128)(2,1)S(1)}, bf16[2,1,56,16,32]{4,2,3,0,1:T(8,128)(2,1)}, bf16[2,1,56,16,32]{4,2,3,0,1:T(8,128)(2,1)}) fusion(f32[2,56,16,64]{3,1,2,0:T(8,128)S(1)} %get-tuple-element.68, f32[56,32]{1,0:T(8,128)S(1)} %get-tuple-element.79, f32[56,32]{1,0:T(8,128)S(1)} %get-tuple-element.78, ...), kind=kLoop, calls=%fused_computation.61 | loop fusion | flops 917504 | bytes 1390592 | tf_op jit(solution)/shard_map/concatenate | solution.py:54
  44.5 1.0 maximum_bitcast_fusion.1
  45.6 2.0 %reshape.290 = bf16[32,28,128]{2,1,0:T(8,128)(2,1)} reshape(bf16[2,16,1,56,64]{4,3,1,0,2:T(8,128)(2,1)} %maximum_bitcast_fusion.1) | data formatting | bytes 458752 | tf_op jit(solution)/shard_map/reshape | solution.py:68
  47.5 8.7 %all-to-all-start.1 = ((bf16[32,28,128]{2,1,0:T(8,128)(2,1)}), bf16[32,28,128]{2,1,0:T(8,128)(2,1)S(1)}, u32[]{:S(2)}, u32[]{:S(2)}) async-start(bf16[32,28,128]{2,1,0:T(8,128)(2,1)} %reshape.290), calls=%async_computation.1 | async-start | bytes 524288 | tf_op jit(solution)/shard_map/all_to_all | solution.py:152
  56.2 2.2 %maximum_bitcast_fusion = bf16[2,16,1,56,64]{4,3,1,0,2:T(8,128)(2,1)} fusion(bf16[2,1,56,16,32]{4,2,3,0,1:T(8,128)(2,1)} %get-tuple-element.76, bf16[2,1,56,16,32]{4,2,3,0,1:T(8,128)(2,1)} %get-tuple-element.77), kind=kLoop, calls=%fused_computation.64 | loop fusion | flops 458752 | bytes 458752 | tf_op jit(solution)/shard_map/transpose | solution.py:65
  58.4 2.0 %reshape.289 = bf16[32,28,128]{2,1,0:T(8,128)(2,1)} reshape(bf16[2,16,1,56,64]{4,3,1,0,2:T(8,128)(2,1)} %maximum_bitcast_fusion) | data formatting | bytes 458752 | tf_op jit(solution)/shard_map/reshape | solution.py:68
  60.4 5.9 %all-to-all-done.1 = bf16[32,28,128]{2,1,0:T(8,128)(2,1)S(1)} async-done(((bf16[32,28,128]{2,1,0:T(8,128)(2,1)}), bf16[32,28,128]{2,1,0:T(8,128)(2,1)S(1)}, u32[]{:S(2)}, u32[]{:S(2)}) %all-to-all-start.1) | async-done | bytes 229408 | tf_op jit(solution)/shard_map/all_to_all | solution.py:152
  66.2 4.2 %all-to-all-start = ((bf16[32,28,128]{2,1,0:T(8,128)(2,1)}), bf16[32,28,128]{2,1,0:T(8,128)(2,1)}, u32[]{:S(2)}, u32[]{:S(2)}) async-start(bf16[32,28,128]{2,1,0:T(8,128)(2,1)} %reshape.289), calls=%async_computation | async-start | bytes 524288 | tf_op jit(solution)/shard_map/all_to_all | solution.py:151
  70.4 2.0 %fusion.30 = bf16[2,16,1,56,64]{4,3,1,0,2:T(8,128)(2,1)} fusion(f32[2,56,3,16,64]{4,1,3,2,0:T(8,128)} %copy-done.2), kind=kLoop, calls=%fused_computation.63 | loop fusion | bytes 458752 | tf_op jit(solution)/shard_map/transpose | solution.py:65
  72.5 2.0 %reshape.292 = bf16[32,28,128]{2,1,0:T(8,128)(2,1)} reshape(bf16[2,16,1,56,64]{4,3,1,0,2:T(8,128)(2,1)} %fusion.30) | data formatting | bytes 458752 | tf_op jit(solution)/shard_map/reshape | solution.py:68
  74.4 6.0 %all-to-all-done = bf16[32,28,128]{2,1,0:T(8,128)(2,1)} async-done(((bf16[32,28,128]{2,1,0:T(8,128)(2,1)}), bf16[32,28,128]{2,1,0:T(8,128)(2,1)}, u32[]{:S(2)}, u32[]{:S(2)}) %all-to-all-start) | async-done | bytes 229408 | tf_op jit(solution)/shard_map/all_to_all | solution.py:151
  80.4 4.4 %all-to-all-start.2 = ((bf16[32,28,128]{2,1,0:T(8,128)(2,1)}), bf16[32,28,128]{2,1,0:T(8,128)(2,1)}, u32[]{:S(2)}, u32[]{:S(2)}) async-start(bf16[32,28,128]{2,1,0:T(8,128)(2,1)} %reshape.292), calls=%async_computation.2 | async-start | bytes 524288 | tf_op jit(solution)/shard_map/all_to_all | solution.py:153
  85.0 0.7 copy.58
  85.7 2.0 %reshape.291 = bf16[2,896,64]{2,1,0:T(8,128)(2,1)} reshape(bf16[2,16,28,128]{3,2,1,0:T(8,128)(2,1)} %bitcast.155) | data formatting | bytes 458752 | tf_op jit(solution)/shard_map/reshape | solution.py:170
  87.7 1.0 copy.59
  88.7 1.0 squeeze.26
  89.7 4.9 %all-to-all-done.2 = bf16[32,28,128]{2,1,0:T(8,128)(2,1)} async-done(((bf16[32,28,128]{2,1,0:T(8,128)(2,1)}), bf16[32,28,128]{2,1,0:T(8,128)(2,1)}, u32[]{:S(2)}, u32[]{:S(2)}) %all-to-all-start.2) | async-done | bytes 229408 | tf_op jit(solution)/shard_map/all_to_all | solution.py:153
  94.7 1.0 copy.57
  95.6 1.0 reshape.293
  96.6 5.7 %fusion.79 = (f32[2,896]{1,0:T(2,128)S(1)}, bf16[2,896,896]{1,2,0:T(8,128)(2,1)}) fusion(pred[896]{0:T(1024)(128)(4,1)S(1)} %lt.36, bf16[2,896,64]{2,1,0:T(8,128)(2,1)} %squeeze.26, bf16[2,896,64]{2,1,0:T(8,128)(2,1)} %reshape.291), kind=kOutput, calls=%fused_computation.224 | convolution fusion | flops 215155584 | bytes 3678080 | tf_op jit(solution)/shard_map/while/body/eval_jaxpr/sub | solution.py:101
  102.4 2.7 %fusion.18 = bf16[2,896,64]{1,2,0:T(8,128)(2,1)S(1)} fusion(bf16[2,896,64]{2,1,0:T(8,128)(2,1)} %reshape.293, bf16[2,896,896]{1,2,0:T(8,128)(2,1)} %get-tuple-element.81, f32[2,896]{1,0:T(2,128)S(1)} %get-tuple-element.80), kind=kOutput, calls=%fused_computation.43 | convolution fusion | flops 205750272 | bytes 3677184 | tf_op jit(solution)/shard_map/while/body/eval_jaxpr/gqk,gkd->gqd/dot_general | solution.py:103
  105.0 1.0 copy.41
  106.0 1.3 reshape_reshape_transpose.3
  107.5 0.9 copy.42
  108.4 4.2 %all-to-all-start.3 = ((bf16[16,2,28,128]{3,1,2,0:T(2,128)(2,1)}), bf16[16,2,28,128]{3,1,2,0:T(2,128)(2,1)}, u32[]{:S(2)}, u32[]{:S(2)}) async-start(bf16[16,2,28,128]{3,1,2,0:T(2,128)(2,1)} %copy.42), calls=%async_computation.3 | async-start | bytes 458752 | tf_op jit(solution)/shard_map/all_to_all | solution.py:174
  114.1 8.0 %all-to-all-done.3 = bf16[16,2,28,128]{3,1,2,0:T(2,128)(2,1)} async-done(((bf16[16,2,28,128]{3,1,2,0:T(2,128)(2,1)}), bf16[16,2,28,128]{3,1,2,0:T(2,128)(2,1)}, u32[]{:S(2)}, u32[]{:S(2)}) %all-to-all-start.3) | async-done | bytes 229408 | tf_op jit(solution)/shard_map/all_to_all | solution.py:174
  122.1 1.0 copy.43
  123.1 1.0 reshape_reshape.2
  124.1 1.9 %copy.44 = bf16[2,1,56,16,64]{4,3,2,0,1:T(8,128)(2,1)} copy(bf16[2,1,56,16,64]{4,2,3,0,1:T(8,128)(2,1)} %bitcast.152) | data formatting | bytes 458752 | tf_op jit(solution)/shard_map/transpose | solution.py:72
  126.0 1.4 %dot_general.28 = bf16[2,56,1024]{2,1,0:T(8,128)(2,1)S(1)} reshape(bf16[2,1,56,16,64]{4,3,2,0,1:T(8,128)(2,1)} %copy.44) | data formatting | bytes 458752 | tf_op jit(solution)/shard_map/dot_general | solution.py:187
  127.4 1.8 %fusion.80 = (f32[2,56]{1,0:T(2,128)S(1)}, f32[2,56,1536]{2,1,0:T(8,128)S(1)}) fusion(f32[2,56,1536]{2,1,0:T(8,128)} %copy-done.1, bf16[2,56,1024]{2,1,0:T(8,128)(2,1)S(1)} %dot_general.28, bf16[1024,1536]{1,0:T(8,128)(2,1)S(1)} %copy-done, f32[1536]{0:T(1024)S(1)} %copy-done.4), kind=kOutput, calls=%fused_computation.225 | convolution fusion | flops 352837504 | bytes 4757952 | tf_op jit(solution)/shard_map/dot_general | solution.py:187
  129.2 0.2 multiply_reduce_fusion
  129.5 0.9 add_convert_fusion.2
  130.4 0.2 fusion.81
  130.7 0.7 copy.46
  131.4 0.7 copy.47
  (43 shorter events, 0.8 us)
Async XLA Ops:
  0.6 126.7 %copy-start = (bf16[1024,1536]{1,0:T(8,128)(2,1)S(1)}, bf16[1024,1536]{1,0:T(8,128)(2,1)}, u32[]{:S(2)}) copy-start(bf16[1024,1536]{1,0:T(8,128)(2,1)} %param.18) | copy-start | bytes 9437188
  3.4 23.6 %collective-permute-start = (bf16[2,15,1536]{2,1,0:T(8,128)(2,1)}, bf16[2,15,1536]{2,1,0:T(8,128)(2,1)}, u32[]{:S(2)}, u32[]{:S(2)}) collective-permute-start(bf16[2,15,1536]{2,1,0:T(8,128)(2,1)} %get-tuple-element.74), channel_id=1, source_target_pairs={{0,1},{1,2},{2,3},{3,4},{4,5},{5,6},{6,7},{7,8},{8,9},{9,10},{10,1... | collective-permute-start | bytes 276488 | tf_op jit(solution)/shard_map/ppermute | solution.py:22
  6.4 20.5 %collective-permute-start.1 = (bf16[2,15,1536]{2,1,0:T(8,128)(2,1)}, bf16[2,15,1536]{2,1,0:T(8,128)(2,1)}, u32[]{:S(2)}, u32[]{:S(2)}) collective-permute-start(bf16[2,15,1536]{2,1,0:T(8,128)(2,1)} %get-tuple-element.75), channel_id=1, source_target_pairs={{1,0},{2,1},{3,2},{4,3},{5,4},{6,5},{7,6},{8,7},{9,8},{10,9},{11,1... | collective-permute-start | bytes 276488 | tf_op jit(solution)/shard_map/ppermute | solution.py:24
  35.2 7.5 %copy-start.1 = (f32[2,56,1536]{2,1,0:T(8,128)}, f32[2,56,1536]{2,1,0:T(8,128)S(1)}, u32[]{:S(2)}) copy-start(f32[2,56,1536]{2,1,0:T(8,128)S(1)} %get-tuple-element.65) | copy-start | bytes 2064388
  42.7 1.8 %copy-start.2 = (f32[2,56,3,16,64]{4,1,3,2,0:T(8,128)}, f32[2,56,3,16,64]{4,1,3,2,0:T(8,128)S(1)}, u32[]{:S(2)}) copy-start(f32[2,56,3,16,64]{4,1,3,2,0:T(8,128)S(1)} %fusion.60) | copy-start | bytes 4128772
  47.5 18.7 %all-to-all-start.1 = ((bf16[32,28,128]{2,1,0:T(8,128)(2,1)}), bf16[32,28,128]{2,1,0:T(8,128)(2,1)S(1)}, u32[]{:S(2)}, u32[]{:S(2)}) async-start(bf16[32,28,128]{2,1,0:T(8,128)(2,1)} %reshape.290), calls=%async_computation.1 | async-start | bytes 524288 | tf_op jit(solution)/shard_map/all_to_all | solution.py:152
  66.2 14.2 %all-to-all-start = ((bf16[32,28,128]{2,1,0:T(8,128)(2,1)}), bf16[32,28,128]{2,1,0:T(8,128)(2,1)}, u32[]{:S(2)}, u32[]{:S(2)}) async-start(bf16[32,28,128]{2,1,0:T(8,128)(2,1)} %reshape.289), calls=%async_computation | async-start | bytes 524288 | tf_op jit(solution)/shard_map/all_to_all | solution.py:151
  80.4 14.2 %all-to-all-start.2 = ((bf16[32,28,128]{2,1,0:T(8,128)(2,1)}), bf16[32,28,128]{2,1,0:T(8,128)(2,1)}, u32[]{:S(2)}, u32[]{:S(2)}) async-start(bf16[32,28,128]{2,1,0:T(8,128)(2,1)} %reshape.292), calls=%async_computation.2 | async-start | bytes 524288 | tf_op jit(solution)/shard_map/all_to_all | solution.py:153
  102.4 10.2 %copy-start.5 = (f32[56,100]{1,0:T(8,128)S(1)}, f32[56,100]{1,0:T(8,128)}, u32[]{:S(2)}) copy-start(f32[56,100]{1,0:T(8,128)} %param.11) | copy-start | bytes 67204
  102.4 25.0 %copy-start.4 = (f32[1536]{0:T(1024)S(1)}, f32[1536]{0:T(1024)}, u32[]{:S(2)}) copy-start(f32[1536]{0:T(1024)} %get-tuple-element.60) | copy-start | bytes 18436
  108.4 13.7 %all-to-all-start.3 = ((bf16[16,2,28,128]{3,1,2,0:T(2,128)(2,1)}), bf16[16,2,28,128]{3,1,2,0:T(2,128)(2,1)}, u32[]{:S(2)}, u32[]{:S(2)}) async-start(bf16[16,2,28,128]{3,1,2,0:T(2,128)(2,1)} %copy.42), calls=%async_computation.3 | async-start | bytes 458752 | tf_op jit(solution)/shard_map/all_to_all | solution.py:174
  127.3 3.0 %copy-start.3 = (bf16[1536,100]{0,1:T(8,128)(2,1)S(1)}, bf16[1536,100]{0,1:T(8,128)(2,1)}, u32[]{:S(2)}) copy-start(bf16[1536,100]{0,1:T(8,128)(2,1)} %param.19) | copy-start | bytes 921604
